TPU v7x, 512 devices: a whole 4x8x8 slice. The times are simulated.
512 devices in a mesh: dp: 128 (over y, z, core), cent: 4 (over x).
Axes of the slice: x: 4, y: 8, z: 8, core: 2. Of those that a mesh axis runs over, the one named last changes fastest.
Arguments:
- frames: bfloat16 [524288, 1024], P(('dp', 'cent')), may hold values from -6 to 6
- video_length: int32 [512, 128], P(('dp', 'cent')), may hold values from 1 to 16, 1024 in all within a row
- video_owner: int32 [512, 128], P(('dp', 'cent')), may hold values from 0 to 127, as said below
- video_cluster: int32 [512, 128], P(('dp', 'cent')), may hold values from 0 to 255
- frame_code: int32 [524288], P(('dp', 'cent')), may hold values from 0 to 8191, as said below
- old_coarse: bfloat16 [32768, 1024], P('dp'), may hold values from -6 to 6
- old_codes: float32 [8192, 1024], P(('dp', 'cent')), may hold values from -6 to 6
Outputs:
- new_coarse: float32 [32768, 1024], P(('dp', 'cent'))
- new_codes: float32 [8192, 1024], P(('dp', 'cent'))
Inputs may be any that keep to these rules, and one draw needn't show every extreme that they name: `video_owner`: each device's row of 128 videos names one index of dp at most 2 times; in every draw some index of dp is named exactly 2 times in every device's row. `frame_code`: among each device's 1024 frames at most 16 have codes in one block of 64 codes (codes b * 64 to (b + 1) * 64 - 1); in every draw some block gets exactly 16 from every device.
All inputs are finite; a program needn't handle non-finite values.
Results may differ from a plain program's by a relative error of at most 0.0015.
Values may be sent and summed in bfloat16 or wider, within the bound.
A program may use at most 64 MiB of HBM per device.

v0:
```python
import jax
import jax.numpy as jnp
from jax import lax
from jax.sharding import PartitionSpec as P

code_prior = 16.0


def cut_along(array, dim, size):
    dims = array.shape
    blocks = array.reshape(*dims[:dim], size, dims[dim] // size, *dims[dim + 1 :])
    return jnp.moveaxis(blocks, dim, 0)


def summed_on_arrival(array, axis, dim):
    blocks = cut_along(array, dim, lax.axis_size(axis))
    arrived = lax.all_to_all(blocks, axis, split_axis=0, concat_axis=0, tiled=True)
    return arrived.sum(axis=0)


def in_one_piece(arrays, axis, dim, along):
    columns = [a.reshape(*a.shape[:along], -1) for a in arrays]
    both = jnp.concatenate(columns, axis=along)
    whole, at, finished = (summed_on_arrival(both, axis, dim), 0, [])
    for a, column in zip(arrays, columns):
        section = whole[..., at : at + column.shape[along]]
        finished.append(section.reshape(*section.shape[:along], *a.shape[along:]))
        at += column.shape[along]
    return tuple(finished)


def copy_for_each(array, axis):
    copies = jnp.broadcast_to(array, (lax.axis_size(axis), *array.shape))
    return lax.all_to_all(copies, axis, split_axis=0, concat_axis=0, tiled=True)


def joined_along(blocks, dim):
    blocks = jnp.moveaxis(blocks, 0, dim)
    dims = blocks.shape
    return blocks.reshape(*dims[:dim], dims[dim] * dims[dim + 1], *dims[dim + 2 :])


def collect(array, axis, dim):
    blocks = copy_for_each(array, axis)
    return joined_along(blocks, dim)


def owner_slots(target, target_count, capacity):
    matches = (target[:, None] == jnp.arange(target_count, dtype=jnp.int32)[None, :]).astype(
        jnp.int32
    )
    before = jnp.cumsum(matches, axis=0) - matches
    slot_rank = jnp.sum(before * matches, axis=1)
    return target * capacity + slot_rank


def invert_slots(slot_list, slot_total):
    item_index = jnp.arange(slot_list.shape[0], dtype=jnp.int32)
    source = jnp.zeros((slot_total,), jnp.int32).at[slot_list].set(item_index)
    filled = jnp.zeros((slot_total,), jnp.int32).at[slot_list].set(1)
    return (source, filled)


def body(frames, video_length, video_owner, video_cluster, frame_code, old_coarse, old_codes):
    dp_count = lax.axis_size("dp")
    cent_count = lax.axis_size("cent")
    frame_count, features = frames.shape
    video_count = video_length.shape[1]
    coarse_rows = old_coarse.shape[0]
    code_share = old_codes.shape[0]
    code_block = code_share * cent_count
    cap_video = max(2, 2 * video_count // dp_count)
    cap_frame = max(2, 2 * frame_count // dp_count)
    lengths = video_length[0]
    target = video_owner[0]
    cluster = video_cluster[0]
    video_ends = jnp.cumsum(lengths)
    video_starts = video_ends - lengths
    position = jnp.arange(frame_count, dtype=jnp.int32)
    member = (
        (position[None, :] >= video_starts[:, None]) & (position[None, :] < video_ends[:, None])
    ).astype(jnp.bfloat16)
    video_sums = jnp.dot(member, frames, preferred_element_type=jnp.float32)
    pooled = (video_sums / lengths[:, None].astype(jnp.float32)).astype(jnp.bfloat16)
    video_slot = owner_slots(target, dp_count, cap_video)
    source, filled = invert_slots(video_slot, dp_count * cap_video)
    send_rows = jnp.where(filled[:, None] > 0, pooled[source], jnp.zeros((), jnp.bfloat16))
    send_codes = jnp.where(filled > 0, cluster[source], -1)
    got_rows, got_codes = (
        lax.all_to_all(
            send_rows.reshape(dp_count, cap_video, features),
            "dp",
            split_axis=0,
            concat_axis=0,
            tiled=True,
        ),
        lax.all_to_all(
            send_codes.reshape(dp_count, cap_video), "dp", split_axis=0, concat_axis=0, tiled=True
        ),
    )
    got_rows = got_rows.reshape(-1, features)
    got_codes = got_codes.reshape(-1)
    table_index = jnp.arange(coarse_rows, dtype=jnp.int32)
    coarse_pick = (got_codes[None, :] == table_index[:, None]).astype(jnp.bfloat16)
    coarse_sum = jnp.dot(coarse_pick, got_rows, preferred_element_type=jnp.float32)
    coarse_count = jnp.sum(coarse_pick.astype(jnp.float32), axis=1)
    quarter = coarse_rows // cent_count
    part_sum, part_count = in_one_piece((coarse_sum, coarse_count), "cent", 0, 1)
    first_row = lax.axis_index("cent") * quarter
    old_part = lax.dynamic_slice_in_dim(old_coarse, first_row, quarter, 0).astype(jnp.float32)
    new_coarse = (part_sum + old_part) / (part_count[:, None] + 1.0)
    anchor_table = collect(new_coarse.astype(jnp.bfloat16), "cent", 0)
    slot_anchor = jnp.dot(coarse_pick.T, anchor_table, preferred_element_type=jnp.float32).astype(
        jnp.bfloat16
    )
    returned = lax.all_to_all(
        slot_anchor.reshape(dp_count, cap_video, features),
        "dp",
        split_axis=0,
        concat_axis=0,
        tiled=True,
    )
    video_anchor = returned.reshape(-1, features)[video_slot]
    frame_anchor = jnp.dot(member.T, video_anchor, preferred_element_type=jnp.float32)
    residual = (frames - frame_anchor).astype(jnp.bfloat16)
    code_target = frame_code // code_block
    code_offset = frame_code - code_target * code_block
    frame_slot = owner_slots(code_target, dp_count, cap_frame)
    source, filled = invert_slots(frame_slot, dp_count * cap_frame)
    slot_rows = jnp.where(filled[:, None] > 0, residual[source], jnp.zeros((), jnp.bfloat16))
    slot_codes = jnp.where(filled > 0, code_offset[source], -1)
    code_rows, code_ids = (
        lax.all_to_all(
            slot_rows.reshape(dp_count, cap_frame, features),
            "dp",
            split_axis=0,
            concat_axis=0,
            tiled=True,
        ),
        lax.all_to_all(
            slot_codes.reshape(dp_count, cap_frame), "dp", split_axis=0, concat_axis=0, tiled=True
        ),
    )
    code_index = jnp.arange(code_block, dtype=jnp.int32)
    code_pick = (code_ids.reshape(-1)[None, :] == code_index[:, None]).astype(jnp.bfloat16)
    code_sum = jnp.dot(
        code_pick, code_rows.reshape(-1, features), preferred_element_type=jnp.float32
    )
    code_count = jnp.sum(code_pick.astype(jnp.float32), axis=1)
    own_sum, own_count = in_one_piece((code_sum, code_count), "cent", 0, 1)
    new_codes = (own_sum + code_prior * old_codes) / (own_count[:, None] + code_prior)
    return (new_coarse, new_codes)


def solution(mesh):
    placed = (
        P(("dp", "cent"), None),
        P(("dp", "cent"), None),
        P(("dp", "cent"), None),
        P(("dp", "cent"), None),
        P(("dp", "cent")),
        P("dp", None),
        P(("dp", "cent"), None),
    )
    return jax.shard_map(
        body,
        mesh=mesh,
        in_specs=placed,
        out_specs=(P(("dp", "cent"), None), P(("dp", "cent"), None)),
        check_vma=False,
    )
```

profile of v0, /device:TPU:49, one launch (start us, length us, event | category | flops | bytes accessed | tf_op | source)
XLA Modules:
  0.0 290.1 jit_solution(10524113724948383758)
XLA Ops:
  0.6 0.7 fusion.26
  1.6 0.8 select_reduce_fusion
  2.4 0.7 fusion.36
  3.1 1.0 scatter_custom_fusion.1
  4.1 1.0 scatter_custom_fusion
  5.1 1.9 gather_fusion
  7.0 0.8 all_to_all.30
  7.7 17.6 %all-to-all-start = ((s32[128,1,2]{2,1,0:T(1,128)}), s32[128,1,2]{2,1,0:T(1,128)S(1)}, u32[]{:S(2)}, u32[]{:S(2)}) async-start(s32[128,1,2]{2,1,0:T(1,128)} %bitcast.5), calls=%async_computation | async-start | bytes 131072 | tf_op jit(solution)/shard_map/all_to_all | solution.py:97
  25.4 0.7 bitcast_convert_fusion
  26.0 0.8 copy.24
  27.1 0.7 bitcast_subtract_fusion.1
  27.7 2.1 fusion
  29.8 1.2 gather_fusion.1
  31.4 1.4 broadcast_select_fusion.1
  32.7 0.9 all-to-all-done
  33.6 13.0 %all-to-all-start.1 = ((bf16[128,2,1024]{2,1,0:T(2,128)(2,1)}), bf16[128,2,1024]{2,1,0:T(2,128)(2,1)S(1)}, u32[]{:S(2)}, u32[]{:S(2)}) async-start(bf16[128,2,1024]{2,1,0:T(2,128)(2,1)} %broadcast_select_fusion.1), calls=%async_computation.1 | async-start | bytes 1048576 | tf_op jit(solution)/shard_map/all_to_all | solution.py:90
  46.6 0.5 broadcast.198
  47.1 0.7 reduce.11
  48.1 0.2 concatenate.16
  48.3 15.4 %all-to-all-done.1 = bf16[128,2,1024]{2,1,0:T(2,128)(2,1)S(1)} async-done(((bf16[128,2,1024]{2,1,0:T(2,128)(2,1)}), bf16[128,2,1024]{2,1,0:T(2,128)(2,1)S(1)}, u32[]{:S(2)}, u32[]{:S(2)}) %all-to-all-start.1) | async-done | bytes 524320 | tf_op jit(solution)/shard_map/all_to_all | solution.py:90
  63.9 0.3 fusion.20
  64.3 1.1 pad_maximum_fusion
  65.4 4.0 %all-to-all-start.2 = ((f32[4,64,1025]{2,1,0:T(8,128)}), f32[4,64,1025]{2,1,0:T(8,128)S(1)}, u32[]{:S(2)}, u32[]{:S(2)}) async-start(f32[4,64,1025]{2,1,0:T(8,128)} %pad_maximum_fusion), calls=%async_computation.2 | async-start | bytes 2359296 | tf_op jit(solution)/shard_map/all_to_all | solution.py:17
  69.5 15.8 %all-to-all-done.2 = f32[4,64,1025]{2,1,0:T(8,128)S(1)} async-done(((f32[4,64,1025]{2,1,0:T(8,128)}), f32[4,64,1025]{2,1,0:T(8,128)S(1)}, u32[]{:S(2)}, u32[]{:S(2)}) %all-to-all-start.2) | async-done | bytes 1049632 | tf_op jit(solution)/shard_map/all_to_all | solution.py:17
  85.5 1.7 fusion.42
  87.2 0.8 broadcast_in_dim.80
  88.1 3.5 %all-to-all-start.4 = ((bf16[4,64,1024]{2,1,0:T(8,128)(2,1)}), bf16[4,64,1024]{2,1,0:T(8,128)(2,1)S(1)}, u32[]{:S(2)}, u32[]{:S(2)}) async-start(bf16[4,64,1024]{2,1,0:T(8,128)(2,1)} %broadcast_in_dim.80), calls=%async_computation.4 | async-start | bytes 1048576 | tf_op jit(solution)/shard_map/all_to_all | solution.py:34
  91.6 0.2 fusion.3
  91.8 7.4 %all-to-all-done.4 = bf16[4,64,1024]{2,1,0:T(8,128)(2,1)S(1)} async-done(((bf16[4,64,1024]{2,1,0:T(8,128)(2,1)}), bf16[4,64,1024]{2,1,0:T(8,128)(2,1)S(1)}, u32[]{:S(2)}, u32[]{:S(2)}) %all-to-all-start.4) | async-done | bytes 524320 | tf_op jit(solution)/shard_map/all_to_all | solution.py:34
  99.3 0.3 convolution_convert_fusion
  99.6 1.0 reshape.180
  100.6 11.0 %all-to-all-start.5 = ((bf16[128,2,1024]{2,1,0:T(2,128)(2,1)}), bf16[128,2,1024]{2,1,0:T(2,128)(2,1)S(1)}, u32[]{:S(2)}, u32[]{:S(2)}) async-start(bf16[128,2,1024]{2,1,0:T(2,128)(2,1)} %reshape.180), calls=%async_computation.5 | async-start | bytes 1048576 | tf_op jit(solution)/shard_map/all_to_all | solution.py:116
  111.7 0.4 fusion.2
  112.1 4.3 %scatter_custom_fusion.3 = s32[2048]{0:T(1024)S(1)} fusion(s32[1024]{0:T(1024)S(1)} %get-tuple-element.8, s32[1024]{0:T(1024)S(1)} %iota.39, s32[]{:T(128)} %constant.19.clone.1), kind=kCustom, calls=%fused_computation.73 | custom fusion | bytes 8196 | tf_op jit(solution)/shard_map/scatter | solution.py:59
  116.5 4.3 %scatter_custom_fusion.2 = s32[2048]{0:T(1024)S(1)} fusion(s32[1024]{0:T(1024)S(1)} %get-tuple-element.8, s32[1024]{0:T(1024)S(1)} %ne.14, s32[]{:T(128)} %constant.19.clone.1), kind=kCustom, calls=%fused_computation.76 | custom fusion | bytes 8196 | tf_op jit(solution)/shard_map/scatter | solution.py:60
  120.8 8.6 %gather_fusion.2 = s32[2048]{0:T(1024)S(1)} fusion(s32[1024]{0:T(1024)S(1)} %get-tuple-element.9, s32[2048]{0:T(1024)S(1)} %fusion.28), kind=kCustom, calls=%fused_computation.2 | custom fusion | bytes 24576 | tf_op jit(solution)/shard_map/gather | solution.py:131
  129.5 0.7 all_to_all.34
  130.2 13.7 %all-to-all-start.3 = ((s32[128,1,16]{2,1,0:T(1,128)}), s32[128,1,16]{2,1,0:T(1,128)S(1)}, u32[]{:S(2)}, u32[]{:S(2)}) async-start(s32[128,1,16]{2,1,0:T(1,128)} %bitcast.12), calls=%async_computation.3 | async-start | bytes 131072 | tf_op jit(solution)/shard_map/all_to_all | solution.py:140
  144.2 0.9 gather_fusion.3
  145.0 2.4 subtract_convert_fusion
  147.5 9.7 %gather_fusion.4 = bf16[2048,1024]{1,0:T(8,128)(2,1)} fusion(bf16[1024,1024]{1,0:T(8,128)(2,1)S(1)} %subtract_convert_fusion, s32[2048]{0:T(1024)S(1)} %fusion.28), kind=kCustom, calls=%fused_computation.4 | custom fusion | bytes 8396800 | tf_op jit(solution)/shard_map/gather | solution.py:130
  157.1 3.7 %broadcast_select_fusion = bf16[128,16,1024]{2,1,0:T(8,128)(2,1)} fusion(bf16[128,16,1024]{2,1,0:T(8,128)(2,1)} %bitcast.39, pred[128,16]{1,0:T(8,128)(4,1)S(1)} %broadcast_in_dim.78), kind=kLoop, calls=%fused_computation.10 | loop fusion | flops 2097152 | bytes 8390656 | tf_op jit(solution)/shard_map/jit(_where)/select_n | solution.py:130
  160.9 14.2 %all-to-all-start.6 = ((bf16[128,16,1024]{2,1,0:T(8,128)(2,1)}), bf16[128,16,1024]{2,1,0:T(8,128)(2,1)}, u32[]{:S(2)}, u32[]{:S(2)}) async-start(bf16[128,16,1024]{2,1,0:T(8,128)(2,1)} %broadcast_select_fusion), calls=%async_computation.6 | async-start | bytes 8388608 | tf_op jit(solution)/shard_map/all_to_all | solution.py:133
  175.1 0.8 reduce.12
  176.2 100.5 %all-to-all-done.6 = bf16[128,16,1024]{2,1,0:T(8,128)(2,1)} async-done(((bf16[128,16,1024]{2,1,0:T(8,128)(2,1)}), bf16[128,16,1024]{2,1,0:T(8,128)(2,1)}, u32[]{:S(2)}, u32[]{:S(2)}) %all-to-all-start.6) | async-done | bytes 4194336 | tf_op jit(solution)/shard_map/all_to_all | solution.py:133
  276.7 3.1 %fusion.7 = f32[4,16,1024]{2,1,0:T(8,128)S(1)} fusion(bf16[2048,1024,1]{1,0,2:T(8,128)(2,1)} %bitcast.16, s32[4,16]{1,0:T(4,128)S(1)} %multiply_add_fusion, s32[2048]{0:T(1024)S(1)} %eq.133), kind=kOutput, calls=%fused_computation.29 | convolution fusion | flops 268566528 | bytes 4464896 | tf_op jit(solution)/shard_map/dot_general | solution.py:146
  279.8 9.4 %all_to_all.48 = f32[4,16,1025]{2,1,0:T(8,128)S(1)} all-to-all(f32[4,16,1025]{2,1,0:T(8,128)S(1)} %pad_maximum_fusion.1), channel_id=1, replica_groups=mesh['dp'=128,'cent'=4] {'cent'}, dimensions={0} | all-to-all | bytes 524800 | tf_op jit(solution)/shard_map/all_to_all | solution.py:17
  289.4 0.7 fusion.25
  (46 shorter events, 2.6 us)
Async XLA Ops:
  0.6 4.4 %copy-start = (s32[1,128]{1,0:T(1,128)S(1)}, s32[1,128]{1,0:T(1,128)}, u32[]{:S(2)}) copy-start(s32[1,128]{1,0:T(1,128)} %param.10) | copy-start | bytes 1540
  7.7 25.9 %all-to-all-start = ((s32[128,1,2]{2,1,0:T(1,128)}), s32[128,1,2]{2,1,0:T(1,128)S(1)}, u32[]{:S(2)}, u32[]{:S(2)}) async-start(s32[128,1,2]{2,1,0:T(1,128)} %bitcast.5), calls=%async_computation | async-start | bytes 131072 | tf_op jit(solution)/shard_map/all_to_all | solution.py:97
  32.7 36.7 %copy-start.2 = (s32[1024]{0:T(1024)S(1)}, s32[1024]{0:T(1024)}, u32[]{:S(2)}) copy-start(s32[1024]{0:T(1024)} %param.11) | copy-start | bytes 12292
  33.6 30.1 %all-to-all-start.1 = ((bf16[128,2,1024]{2,1,0:T(2,128)(2,1)}), bf16[128,2,1024]{2,1,0:T(2,128)(2,1)S(1)}, u32[]{:S(2)}, u32[]{:S(2)}) async-start(bf16[128,2,1024]{2,1,0:T(2,128)(2,1)} %broadcast_select_fusion.1), calls=%async_computation.1 | async-start | bytes 1048576 | tf_op jit(solution)/shard_map/all_to_all | solution.py:90
  65.4 19.9 %all-to-all-start.2 = ((f32[4,64,1025]{2,1,0:T(8,128)}), f32[4,64,1025]{2,1,0:T(8,128)S(1)}, u32[]{:S(2)}, u32[]{:S(2)}) async-start(f32[4,64,1025]{2,1,0:T(8,128)} %pad_maximum_fusion), calls=%async_computation.2 | async-start | bytes 2359296 | tf_op jit(solution)/shard_map/all_to_all | solution.py:17
  88.1 11.2 %all-to-all-start.4 = ((bf16[4,64,1024]{2,1,0:T(8,128)(2,1)}), bf16[4,64,1024]{2,1,0:T(8,128)(2,1)S(1)}, u32[]{:S(2)}, u32[]{:S(2)}) async-start(bf16[4,64,1024]{2,1,0:T(8,128)(2,1)} %broadcast_in_dim.80), calls=%async_computation.4 | async-start | bytes 1048576 | tf_op jit(solution)/shard_map/all_to_all | solution.py:34
  100.6 29.6 %all-to-all-start.5 = ((bf16[128,2,1024]{2,1,0:T(2,128)(2,1)}), bf16[128,2,1024]{2,1,0:T(2,128)(2,1)S(1)}, u32[]{:S(2)}, u32[]{:S(2)}) async-start(bf16[128,2,1024]{2,1,0:T(2,128)(2,1)} %reshape.180), calls=%async_computation.5 | async-start | bytes 1048576 | tf_op jit(solution)/shard_map/all_to_all | solution.py:116
  130.2 30.6 %all-to-all-start.3 = ((s32[128,1,16]{2,1,0:T(1,128)}), s32[128,1,16]{2,1,0:T(1,128)S(1)}, u32[]{:S(2)}, u32[]{:S(2)}) async-start(s32[128,1,16]{2,1,0:T(1,128)} %bitcast.12), calls=%async_computation.3 | async-start | bytes 131072 | tf_op jit(solution)/shard_map/all_to_all | solution.py:140
  160.9 115.9 %all-to-all-start.6 = ((bf16[128,16,1024]{2,1,0:T(8,128)(2,1)}), bf16[128,16,1024]{2,1,0:T(8,128)(2,1)}, u32[]{:S(2)}, u32[]{:S(2)}) async-start(bf16[128,16,1024]{2,1,0:T(8,128)(2,1)} %broadcast_select_fusion), calls=%async_computation.6 | async-start | bytes 8388608 | tf_op jit(solution)/shard_map/all_to_all | solution.py:133
  175.1 114.3 %copy-start.1 = (f32[16,1024]{1,0:T(8,128)S(1)}, f32[16,1024]{1,0:T(8,128)}, u32[]{:S(2)}) copy-start(f32[16,1024]{1,0:T(8,128)} %param.13) | copy-start | bytes 196612
where the time goes:
time: 291 us; the launch traced here: 290 us
  waiting for transfers between devices  140 us (48%)
  starting transfers between devices  77 us (26%)
  local copies, waits for them, and re-layouts  38.9 us (13%)
  other arithmetic  15.4 us (5%)
  blocking collectives  9.43 us (3%)
  matrix products  8.26 us (3%)
    all_to_all x1, waiting for transfers between devices, body(): lax.all_to_all(slot_rows.reshape(dp_count, cap_frame, features), 'dp', sp...  100 us
    all_to_all x1, starting transfers between devices, body(): lax.all_to_all(send_codes.reshape(dp_count, cap_video), 'dp', split_axis=...  17.6 us
    all_to_all x1, waiting for transfers between devices, summed_on_arrival(): lax.all_to_all(blocks, axis, split_axis=0, concat_axis=0, tiled=True)  15.8 us
    all_to_all x1, waiting for transfers between devices, body(): lax.all_to_all(send_rows.reshape(dp_count, cap_video, features), 'dp', sp...  15.4 us
    all_to_all x1, starting transfers between devices, body(): lax.all_to_all(slot_rows.reshape(dp_count, cap_frame, features), 'dp', sp...  14.2 us
    all_to_all x1, starting transfers between devices, body(): lax.all_to_all(slot_codes.reshape(dp_count, cap_frame), 'dp', split_axis=...  13.7 us
    all_to_all x1, starting transfers between devices, body(): lax.all_to_all(send_rows.reshape(dp_count, cap_video, features), 'dp', sp...  13 us
    all_to_all x1, starting transfers between devices, body(): lax.all_to_all(slot_anchor.reshape(dp_count, cap_video, features), 'dp',...  11 us
  transfers between devices with their start and end apart: 7, of which 5 were waited for; matrix products, arithmetic and copies ran while one was open for 16% of the time, Pallas kernels for 0%

commit v1 on v0

v1 whole, which is shorter than its diff:
```python
import jax
import jax.numpy as jnp
from jax import lax
from jax.experimental import pallas as pl
from jax.experimental.pallas import tpu as pltpu
from jax.sharding import PartitionSpec as P

code_prior = 16.0
NL = 8
NY = 8
NZ = 8
W = 128
F32 = jnp.float32
BF16 = jnp.bfloat16


def iota(shape, dim):
    return lax.broadcasted_iota(jnp.int32, shape, dim).astype(F32)


def hot(condition):
    return jnp.where(condition, 1.0, 0.0).astype(BF16)


def columns(row):
    return jnp.transpose(jnp.broadcast_to(row, (128, 128)))


def dot(a, b):
    return jnp.dot(a, b, preferred_element_type=F32)


def dot_t(a, b):
    return lax.dot_general(a, b, (((1,), (1,)), ((), ())), preferred_element_type=F32)


def kernel(
    frames_ref, length_ref, owner_ref, cluster_ref, code_ref, old_ref, old_codes_ref,
    coarse_out, codes_out,
    frames_v, mine, theirs, pooled, pool_in, old_v,
    meta, metas, both, rows, picks, words,
    send_c, hop_c, got_c, back_0, back_1, back_2,
    note_0, note_1, note_s, note_2, fresh, fresh_in,
    table, table_1, part, part_2, last, last_in, count, count_in, column,
    load_sem, xs, xr, fs, fr, ps, pr, ns, nr, cs, cr, bs, br, ts, tr, es, er,
):
    dp = lax.axis_index("dp")
    x = lax.axis_index("cent")
    c = lax.rem(dp, 2)
    z = lax.rem(lax.div(dp, 2), NZ)
    y = lax.div(dp, 2 * NZ)
    m = x * 2 + c
    here = (y, z)

    def member(d):
        other = lax.rem(m + d, NL)
        return other, {"dp": (y * NZ + z) * 2 + lax.rem(other, 2), "cent": lax.div(other, 2)}

    def on_y(d):
        other = lax.rem(y + d, NY)
        return other, {"dp": (other * NZ + z) * 2 + c, "cent": x}

    def on_z(d):
        other = lax.rem(z + d, NZ)
        return other, {"dp": (y * NZ + other) * 2 + c, "cent": x}

    on = (on_y, on_z)

    def remote(src, dst, send, recv, target):
        copy = pltpu.make_async_remote_copy(
            src_ref=src, dst_ref=dst, send_sem=send, recv_sem=recv,
            device_id=target, device_id_type=pl.DeviceIdType.MESH,
        )
        copy.start()
        return copy

    def local(src, dst, sem):
        copy = pltpu.make_async_copy(src, dst, sem)
        copy.start()
        return copy

    def wait(copies):
        for copy in copies:
            copy.wait()

    def spread(src, dst, send, recv, stage, axis):
        copies = []
        for d in range(1, 8):
            other, target = on[axis](d)
            copies.append(remote(src(other), dst, send.at[stage, d], recv.at[stage, d], target))
        return copies

    barrier = pltpu.get_barrier_semaphore()
    for d in range(1, 8):
        for find in (member, on_y, on_z):
            pl.semaphore_signal(
                barrier, inc=1, device_id=find(d)[1], device_id_type=pl.DeviceIdType.MESH
            )

    my_lanes = pl.ds(pl.multiple_of(m * W, W), W)
    load = local(frames_ref, frames_v, load_sem.at[0])
    load_mine = local(frames_ref.at[:, my_lanes], theirs.at[m], load_sem.at[1])
    load_old = local(old_ref.at[:, my_lanes], old_v.at[c], load_sem.at[2])

    sub128, lane128 = iota((128, 128), 0), iota((128, 128), 1)
    sub64 = iota((64, 128), 0)
    length = length_ref[...].astype(F32)
    through = hot(sub128 <= lane128)
    before = hot(sub128 < lane128)
    ends_row = dot(jnp.broadcast_to(length, (8, 128)).astype(BF16), through)[0:1]
    ends = columns(ends_row)
    lengths = columns(length)
    starts = ends - lengths
    pieces = []
    for a in range(8):
        position = lane128 + 128.0 * a
        pieces.append(hot(jnp.logical_and(position >= starts, position < ends)))
        meta[16 + a : 17 + a, :] = jnp.sum(
            jnp.where(ends <= position, 1.0, 0.0), axis=0, keepdims=True
        )
    of_video = jnp.concatenate(pieces, axis=1)

    owner_int = owner_ref[...]
    owner = owner_int.astype(F32)
    same = jnp.logical_and(columns(owner) == owner, sub128 < lane128)
    repeat = jnp.sum(jnp.where(same, 1.0, 0.0), axis=0, keepdims=True)
    half = jnp.bitwise_and(owner_int, 1)
    to_y = jnp.right_shift(owner_int, 4)
    to_z = jnp.bitwise_and(jnp.right_shift(owner_int, 1), NZ - 1)
    place = jnp.where(half == 0, to_y * NZ + to_z, to_z * NY + to_y)
    meta[32:33, :] = (half * 1024 + place * 16).astype(F32) + repeat
    meta[33:34, :] = cluster_ref[...].astype(F32) + 1.0
    meta[34:35, :] = place.astype(F32)
    meta[35:36, :] = repeat
    meta[36:37, :] = half.astype(F32)
    meta[37:40, :] = jnp.zeros((3, 128), F32)

    codes = code_ref[...]
    line_of = jnp.right_shift(codes, 7).astype(F32)
    in_line = jnp.bitwise_and(codes, 127).astype(F32)
    ones = jnp.ones((128, 128), BF16)
    seen = jnp.zeros((64, 128), F32)
    histogram = jnp.zeros((64, 128), F32)
    for a in range(8):
        match = hot(line_of[a : a + 1] == sub64)
        rank = jnp.sum(
            match.astype(F32) * (dot(match, before) + seen), axis=0, keepdims=True
        )
        meta[a : a + 1, :] = line_of[a : a + 1] * 32.0 + rank
        seen = seen + dot(match, ones)
        histogram = histogram + dot_t(match, hot(in_line[a : a + 1] == sub128))
    meta[8:16, :] = in_line
    meta[24:32, :] = line_of
    metas[pl.ds(m, 1)] = meta[...].reshape(1, 40, 128)
    for j in range(8):
        note_0[0, j, 0:8, :] = histogram[8 * j : 8 * j + 8]
        note_0[1, j, 0:8, :] = jnp.zeros((8, 128), F32)

    pl.semaphore_wait(barrier, 21)
    x_copies, f_copies, p_copies = [], [], []
    for d in range(1, 8):
        other, target = member(d)
        x_copies.append(remote(meta, metas.at[m], xs.at[d], xr.at[d], target))
    partner = lax.rem(c + 1, 2)
    old_copy = remote(
        old_ref.at[:, pl.ds(pl.multiple_of((x * 2 + partner) * W, W), W)],
        old_v.at[c], xs.at[0], xr.at[0],
        {"dp": (y * NZ + z) * 2 + partner, "cent": x},
    )
    load.wait()
    for j in range(8):
        part_sum = dot(of_video, frames_v[:, 128 * j : 128 * j + 128])
        pooled[j] = (part_sum / lengths).astype(BF16)
    for d in range(1, 8):
        other, target = member(d)
        p_copies.append(
            remote(pooled.at[other], pool_in.at[m], ps.at[d], pr.at[d], target)
        )
    for d in range(1, 8):
        other, target = member(d)
        lanes = pl.ds(pl.multiple_of(other * W, W), W)
        f_copies.append(
            remote(frames_ref.at[:, lanes], theirs.at[m], fs.at[d], fr.at[d], target)
        )
    pool_in[pl.ds(m, 1)] = pooled[pl.ds(m, 1)]

    wait(x_copies)
    note = [jnp.zeros((64, 128), F32), jnp.zeros((64, 128), F32)]
    for s in range(NL):
        info = metas[s, 32:40, :]
        value = info[1:2]
        at = jnp.where(info[2:3] == sub64, value, 0.0)
        for h in range(2):
            chosen = jnp.where(info[4:5] == float(h), at, 0.0).astype(BF16)
            lane = hot(info[3:4] + (here[h] * 16 + 2 * s).astype(F32) == sub128)
            note[h] = note[h] + dot_t(chosen, lane)
    for h in range(2):
        for j in range(8):
            note_0[h, j, 8:16, :] = note[h][8 * j : 8 * j + 8]
    n_copies = []
    for h in range(2):
        n_copies += spread(lambda o: note_0.at[h, o], note_1.at[h, here[h]], ns, nr, h, h)
        note_1[h, pl.ds(here[h], 1)] = note_0[h, pl.ds(here[h], 1)]

    wait(p_copies)
    sub256 = iota((256, 128), 0)

    def fill(chunk, carry):
        shift = (chunk * 256).astype(F32)
        pick = jnp.concatenate(
            [hot(metas[s, 32:33, :] + 2.0 * s - shift == sub256) for s in range(NL)], axis=1
        )
        filled = dot(pick, pool_in[...].reshape(1024, W))
        send_c[pl.ds(chunk * 16, 16)] = filled.astype(BF16).reshape(16, 16, W)
        return carry

    lax.fori_loop(0, 8, fill, 0)
    c_copies = []
    for h in range(2):
        c_copies += spread(
            lambda o: send_c.at[pl.ds(64 * h + 8 * o, 8)], hop_c.at[h, here[h]], cs, cr, h, h
        )
        hop_c[h, pl.ds(here[h], 1)] = send_c[pl.ds(64 * h + 8 * here[h], 8)].reshape(1, 8, 16, W)

    wait(n_copies)
    for h in range(2):
        note_s[h] = jnp.sum(note_1[h], axis=0)
    n_copies = []
    for h in range(2):
        n_copies += spread(
            lambda o: note_s.at[h], note_2.at[h, here[1 - h]], ns, nr, 2 + h, 1 - h
        )
        note_2[h, pl.ds(here[1 - h], 1)] = note_s[h].reshape(1, 16, 128)

    def take(d):
        s = lax.rem(m + NL - d, NL)
        for a in range(8):
            both[128 * a : 128 * a + 128, W:] = hot(
                columns(metas[s, 16 + a : 17 + a, :]) == lane128
            )
        both[:, :W] = theirs[s]

        def chunk_of(chunk, carry):
            shift = (chunk * 256).astype(F32)
            pick = jnp.concatenate(
                [hot(metas[s, a : a + 1, :] - shift == sub256) for a in range(8)], axis=1
            )
            out = dot(pick, both[...]).astype(BF16)
            rows[s, pl.ds(chunk * 8, 8)] = out[:, :W].reshape(8, 32, W)
            picks[s, pl.ds(chunk * 8, 8)] = out[:, W:].reshape(8, 32, W)
            return carry

        lax.fori_loop(0, 8, chunk_of, 0)

    def arrive(d):
        if d == 0:
            load_mine.wait()
        else:
            f_copies[d - 1].wait()
        take(d)

    def word(s, carry):
        total = jnp.zeros((64, 128), F32)
        offset = (lax.rem(s, 4) * 32).astype(F32)
        for a in range(8):
            line = metas[s, 24 + a : 25 + a, :]
            rank = metas[s, a : a + 1, :] - 32.0 * line + offset
            value = metas[s, 8 + a : 9 + a, :] + 1.0
            total = total + dot_t(
                jnp.where(line == sub64, value, 0.0).astype(BF16), hot(rank == sub128)
            )
        group = pl.ds(lax.div(s, 4), 1)
        words[group] = words[group] + total.reshape(1, 64, 128)
        return carry

    arrive(0)
    arrive(1)

    wait(c_copies)
    c_copies = []
    for h in range(2):
        c_copies += spread(
            lambda o: hop_c.at[h, :, o], got_c.at[h, here[1 - h]], cs, cr, 2 + h, 1 - h
        )
        got_c[h, pl.ds(here[1 - h], 1)] = hop_c[h, :, pl.ds(here[1 - h], 1)].reshape(1, 8, 16, W)
    words[...] = jnp.zeros((2, 64, 128), F32)
    lax.fori_loop(0, NL, word, 0)
    arrive(2)
    wait(n_copies)
    load_old.wait()
    old_copy.wait()
    wait(c_copies)

    sub8 = iota((8, 128), 0)
    b_copies, v_copies = [], []
    for h in range(2):
        mask = sub8 == here[1 - h].astype(F32)
        ids = [
            jnp.sum(jnp.where(mask, note_2[h, j, 8:16, :], 0.0), axis=0, keepdims=True)
            for j in range(8)
        ]
        pick = jnp.concatenate([hot(ids[j] == sub256 + 1.0) for j in range(8)], axis=1)
        total = dot(pick, got_c[h].reshape(1024, W))
        amount = dot(pick, jnp.ones((1024, W), BF16))
        new = (total + old_v[h].astype(F32)) / (amount + 1.0)
        for q in range(4):
            fresh[2 * q + h] = new[64 * q : 64 * q + 64]
        anchor = new.astype(BF16)
        lane256 = iota((128, 256), 1)
        for j in range(8):
            column_of = columns(ids[j])
            back = hot(jnp.concatenate([column_of, column_of], axis=1) == lane256 + 1.0)
            back_0[h, j] = dot(back, anchor).astype(BF16).reshape(8, 16, W)
        b_copies += spread(
            lambda o: back_0.at[h, o], back_1.at[h, here[1 - h]], bs, br, h, 1 - h
        )
        back_1[h, pl.ds(here[1 - h], 1)] = back_0[h, pl.ds(here[1 - h], 1)]
    counts = jnp.zeros((1, 128), F32)
    for j in range(8):
        counts = counts + jnp.sum(
            jnp.where(sub8 == z.astype(F32), note_2[0, j, 0:8, :], 0.0), axis=0, keepdims=True
        )
    count[...] = jnp.broadcast_to(counts, (8, 128))
    count_in[pl.ds(m, 1)] = count[...].reshape(1, 8, 128)
    for d in range(1, 8):
        other, target = member(d)
        v_copies.append(
            remote(fresh.at[other], fresh_in.at[m], es.at[0, d], er.at[0, d], target)
        )
        v_copies.append(
            remote(count, count_in.at[m], es.at[1, d], er.at[1, d], target)
        )
    fresh_in[pl.ds(m, 1)] = fresh[pl.ds(m, 1)]
    arrive(3)
    arrive(4)

    wait(b_copies)
    b_copies = []
    for h in range(2):
        b_copies += spread(
            lambda o: back_1.at[h, :, o], back_2.at[h, here[h]], bs, br, 2 + h, h
        )
        back_2[h, pl.ds(here[h], 1)] = back_1[h, :, pl.ds(here[h], 1)].reshape(1, 8, 16, W)
    arrive(5)
    arrive(6)
    arrive(7)
    wait(b_copies)

    def subtract(s, carry):
        wanted = columns(metas[s, 32:33, :] + (2 * s).astype(F32))
        pick = jnp.concatenate([hot(wanted == lane128 + 128.0 * t) for t in range(16)], axis=1)
        anchor = dot(pick, back_2[...].reshape(2048, W)).astype(BF16)

        def chunk_of(chunk, inner):
            at = pl.ds(chunk * 8, 8)
            near = dot(picks[s, at].reshape(256, W), anchor)
            left = rows[s, at].reshape(256, W).astype(F32) - near
            rows[s, at] = left.astype(BF16).reshape(8, 32, W)
            return inner

        return lax.fori_loop(0, 8, chunk_of, carry)

    lax.fori_loop(0, NL, subtract, 0)

    def tabulate(k, carry):
        pick = jnp.concatenate(
            [hot(words[g, pl.ds(k, 1), :] == sub128 + 1.0) for g in range(2)], axis=1
        )
        sums = dot(pick, rows[:, pl.ds(k, 1)].reshape(256, W)).astype(BF16)
        across = lax.rem(k, 8) * 8 + lax.div(k, 8)
        table[0, pl.ds(k, 1)] = sums[0:64].reshape(1, 64, W)
        table[1, pl.ds(across, 1)] = sums[64:128].reshape(1, 64, W)
        return carry

    lax.fori_loop(0, 64, tabulate, 0)
    t_copies = []
    for h in range(2):
        t_copies += spread(
            lambda o: table.at[h, pl.ds(8 * o, 8)], table_1.at[h, here[h]], ts, tr, h, h
        )
        table_1[h, pl.ds(here[h], 1)] = table[h, pl.ds(8 * here[h], 8)].reshape(1, 8, 64, W)
    wait(v_copies)
    for s in range(NL):
        coarse_out[:, W * s : W * s + W] = fresh_in[s]
    column[...] = columns(jnp.sum(count_in[...], axis=0)[0:1])
    wait(t_copies)

    def gather(j, carry):
        for h in range(2):
            total = jnp.zeros((64, W), F32)
            for i in range(8):
                total = total + table_1[h, i, pl.ds(j, 1)].reshape(64, W).astype(F32)
            part[h, pl.ds(j, 1)] = total.reshape(1, 64, W)
        return carry

    lax.fori_loop(0, 8, gather, 0)
    t_copies = []
    for h in range(2):
        t_copies += spread(
            lambda o: part.at[h, o], part_2.at[h, here[1 - h]], ts, tr, 2 + h, 1 - h
        )
        part_2[h, pl.ds(here[1 - h], 1)] = part[h, pl.ds(here[1 - h], 1)]
    wait(t_copies)
    for h in range(2):
        total = jnp.sum(part_2[h], axis=0)
        for q in range(4):
            last[2 * q + h] = total[16 * q : 16 * q + 16]
    e_copies = []
    for d in range(1, 8):
        other, target = member(d)
        e_copies.append(
            remote(last.at[other], last_in.at[m], es.at[2, d], er.at[2, d], target)
        )
    last_in[pl.ds(m, 1)] = last[pl.ds(m, 1)]
    mine[...] = column[pl.ds(pl.multiple_of(c * 64 + x * 16, 16), 16), :] + code_prior
    wait(e_copies)
    for s in range(NL):
        lanes = slice(W * s, W * s + W)
        codes_out[:, lanes] = (last_in[s] + code_prior * old_codes_ref[:, lanes]) / mine[...]


def body(frames, video_length, video_owner, video_cluster, frame_code, old_coarse, old_codes):
    dma = pltpu.SemaphoreType.DMA
    vmem = pl.BlockSpec(memory_space=pltpu.VMEM)
    hbm = pl.BlockSpec(memory_space=pl.ANY)
    return pl.pallas_call(
        kernel,
        out_shape=(
            jax.ShapeDtypeStruct((64, 1024), F32),
            jax.ShapeDtypeStruct((16, 1024), F32),
        ),
        in_specs=[hbm, vmem, vmem, vmem, vmem, hbm, vmem],
        out_specs=(vmem, vmem),
        scratch_shapes=[
            pltpu.VMEM((1024, 1024), BF16),
            pltpu.VMEM((16, 128), F32),
            pltpu.VMEM((NL, 1024, W), BF16),
            pltpu.VMEM((NL, 128, W), BF16),
            pltpu.VMEM((NL, 128, W), BF16),
            pltpu.VMEM((2, 256, W), BF16),
            pltpu.VMEM((40, 128), F32),
            pltpu.VMEM((NL, 40, 128), F32),
            pltpu.VMEM((1024, 2 * W), BF16),
            pltpu.VMEM((NL, 64, 32, W), BF16),
            pltpu.VMEM((NL, 64, 32, W), BF16),
            pltpu.VMEM((2, 64, 128), F32),
            pltpu.VMEM((128, 16, W), BF16),
            pltpu.VMEM((2, 8, 8, 16, W), BF16),
            pltpu.VMEM((2, 8, 8, 16, W), BF16),
            pltpu.VMEM((2, 8, 8, 16, W), BF16),
            pltpu.VMEM((2, 8, 8, 16, W), BF16),
            pltpu.VMEM((2, 8, 8, 16, W), BF16),
            pltpu.VMEM((2, 8, 16, 128), F32),
            pltpu.VMEM((2, 8, 16, 128), F32),
            pltpu.VMEM((2, 16, 128), F32),
            pltpu.VMEM((2, 8, 16, 128), F32),
            pltpu.VMEM((NL, 64, W), F32),
            pltpu.VMEM((NL, 64, W), F32),
            pltpu.VMEM((2, 64, 64, W), BF16),
            pltpu.VMEM((2, 8, 8, 64, W), BF16),
            pltpu.VMEM((2, 8, 64, W), F32),
            pltpu.VMEM((2, 8, 64, W), F32),
            pltpu.VMEM((NL, 16, W), F32),
            pltpu.VMEM((NL, 16, W), F32),
            pltpu.VMEM((8, 128), F32),
            pltpu.VMEM((NL, 8, 128), F32),
            pltpu.VMEM((128, 128), F32),
            dma((3,)),
            dma((8,)), dma((8,)),
            dma((8,)), dma((8,)),
            dma((8,)), dma((8,)),
            dma((4, 8)), dma((4, 8)),
            dma((4, 8)), dma((4, 8)),
            dma((4, 8)), dma((4, 8)),
            dma((4, 8)), dma((4, 8)),
            dma((3, 8)), dma((3, 8)),
        ],
        compiler_params=pltpu.CompilerParams(
            collective_id=0, has_side_effects=True, vmem_limit_bytes=56 << 20
        ),
    )(
        frames, video_length, video_owner, video_cluster,
        frame_code.reshape(8, 128), old_coarse, old_codes,
    )


def solution(mesh):
    placed = (
        P(("dp", "cent"), None),
        P(("dp", "cent"), None),
        P(("dp", "cent"), None),
        P(("dp", "cent"), None),
        P(("dp", "cent")),
        P("dp", None),
        P(("dp", "cent"), None),
    )
    return jax.shard_map(
        body,
        mesh=mesh,
        in_specs=placed,
        out_specs=(P(("dp", "cent"), None), P(("dp", "cent"), None)),
        check_vma=False,
    )
```

time: 291 us -> 132 us (0.45)
  the two profiles are of different devices: /device:TPU:49 before, /device:TPU:1 now
where the time goes in v1:
time: 132 us
  Pallas kernels  128 us (97%)
  local copies, waits for them, and re-layouts  3.14 us (2%)
    pallas_call x1, Pallas kernels, body(): pl.pallas_call(kernel, out_shape=(jax.ShapeDtypeStruct((64, 1024), F32),...  128 us
    unnamed x2, local copies, waits for them, and re-layouts  3.14 us

profile of v1, /device:TPU:1, one launch (start us, length us, event | category | flops | bytes accessed | tf_op | source)
XLA Modules:
  0.0 132.2 jit_solution(1353316992150681786)
XLA Ops:
  0.6 128.4 %shard_map.86 = (f32[64,1024]{1,0:T(8,128)}, f32[16,1024]{1,0:T(8,128)}) custom-call(bf16[1024,1024]{1,0:T(8,128)(2,1)} %frames_ref.1, s32[1,128]{1,0:T(1,128)} %length_ref.1, s32[1,128]{1,0:T(1,128)} %owner_ref.1, s32[1,128]{1,0:T(1,128)} %cluster_ref.1, s32[8,128]{1,0:T(8,128)} %bitcast.1, bf16[256,1024]{1,0:T(8,128)(2,1)} %old_ref.1, f32[16,1024]{1,0:T(8,128)} %old_codes_ref.1), custom_call_target="tpu_custom_call" | custom-call | tf_op jit(solution)/shard_map/pallas_call | solution.py:426
  129.1 1.7 %copy.11 = f32[64,1024]{1,0:T(8,128)} copy(f32[64,1024]{1,0:T(8,128)} %get-tuple-element.4) | data formatting | bytes 524288
  130.7 1.5 %copy.12 = f32[16,1024]{1,0:T(8,128)} copy(f32[16,1024]{1,0:T(8,128)} %get-tuple-element.5) | data formatting | bytes 131072

commit v2 on v1

--- a/solution.py
+++ b/solution.py
@@ -38,7 +38,7 @@
     frames_ref, length_ref, owner_ref, cluster_ref, code_ref, old_ref, old_codes_ref,
     coarse_out, codes_out,
     frames_v, mine, theirs, pooled, pool_in, old_v,
-    meta, metas, both, rows, picks, words,
+    meta, metas, both, rows, picks, rest, words, wants, anchors,
     send_c, hop_c, got_c, back_0, back_1, back_2,
     note_0, note_1, note_s, note_2, fresh, fresh_in,
     table, table_1, part, part_2, last, last_in, count, count_in, column,
@@ -66,12 +66,13 @@
 
     on = (on_y, on_z)
 
-    def remote(src, dst, send, recv, target):
+    def remote(src, dst, send, recv, target, start=True):
         copy = pltpu.make_async_remote_copy(
             src_ref=src, dst_ref=dst, send_sem=send, recv_sem=recv,
             device_id=target, device_id_type=pl.DeviceIdType.MESH,
         )
-        copy.start()
+        if start:
+            copy.start()
         return copy
 
     def local(src, dst, sem):
@@ -156,6 +157,10 @@
         note_0[0, j, 0:8, :] = histogram[8 * j : 8 * j + 8]
         note_0[1, j, 0:8, :] = jnp.zeros((8, 128), F32)
 
+    load.wait()
+    for j in range(8):
+        part_sum = dot(of_video, frames_v[:, 128 * j : 128 * j + 128])
+        pooled[j] = (part_sum / lengths).astype(BF16)
     pl.semaphore_wait(barrier, 21)
     x_copies, f_copies, p_copies = [], [], []
     for d in range(1, 8):
@@ -167,10 +172,6 @@
         old_v.at[c], xs.at[0], xr.at[0],
         {"dp": (y * NZ + z) * 2 + partner, "cent": x},
     )
-    load.wait()
-    for j in range(8):
-        part_sum = dot(of_video, frames_v[:, 128 * j : 128 * j + 128])
-        pooled[j] = (part_sum / lengths).astype(BF16)
     for d in range(1, 8):
         other, target = member(d)
         p_copies.append(
@@ -185,15 +186,19 @@
     pool_in[pl.ds(m, 1)] = pooled[pl.ds(m, 1)]
 
     wait(x_copies)
-    note = [jnp.zeros((64, 128), F32), jnp.zeros((64, 128), F32)]
-    for s in range(NL):
-        info = metas[s, 32:40, :]
-        value = info[1:2]
-        at = jnp.where(info[2:3] == sub64, value, 0.0)
-        for h in range(2):
-            chosen = jnp.where(info[4:5] == float(h), at, 0.0).astype(BF16)
-            lane = hot(info[3:4] + (here[h] * 16 + 2 * s).astype(F32) == sub128)
-            note[h] = note[h] + dot_t(chosen, lane)
+    places, values, halves, repeats = [
+        [metas[s, i : i + 1, :] for s in range(NL)] for i in (34, 33, 36, 35)
+    ]
+    note = []
+    for h in range(2):
+        chosen = [
+            jnp.where(
+                jnp.logical_and(places[s] == sub64, halves[s] == float(h)), values[s], 0.0
+            ).astype(BF16)
+            for s in range(NL)
+        ]
+        lane = [hot(repeats[s] + (here[h] * 16 + 2 * s).astype(F32) == sub128) for s in range(NL)]
+        note.append(dot_t(jnp.concatenate(chosen, axis=1), jnp.concatenate(lane, axis=1)))
     for h in range(2):
         for j in range(8):
             note_0[h, j, 8:16, :] = note[h][8 * j : 8 * j + 8]
@@ -260,21 +265,29 @@
         take(d)
 
     def word(s, carry):
-        total = jnp.zeros((64, 128), F32)
         offset = (lax.rem(s, 4) * 32).astype(F32)
+        values, ranks = [], []
         for a in range(8):
             line = metas[s, 24 + a : 25 + a, :]
             rank = metas[s, a : a + 1, :] - 32.0 * line + offset
             value = metas[s, 8 + a : 9 + a, :] + 1.0
-            total = total + dot_t(
-                jnp.where(line == sub64, value, 0.0).astype(BF16), hot(rank == sub128)
-            )
+            values.append(jnp.where(line == sub64, value, 0.0).astype(BF16))
+            ranks.append(hot(rank == sub128))
+        total = dot_t(jnp.concatenate(values, axis=1), jnp.concatenate(ranks, axis=1))
         group = pl.ds(lax.div(s, 4), 1)
         words[group] = words[group] + total.reshape(1, 64, 128)
         return carry
 
+    def choose(s, carry):
+        wanted = columns(metas[s, 32:33, :] + (2 * s).astype(F32))
+        pick = [hot(wanted == lane128 + 128.0 * t) for t in range(16)]
+        wants[pl.ds(pl.multiple_of(s * 128, 128), 128), :] = jnp.concatenate(pick, axis=1)
+        return carry
+
     arrive(0)
-    arrive(1)
+    words[...] = jnp.zeros((2, 64, 128), F32)
+    lax.fori_loop(0, NL, word, 0)
+    lax.fori_loop(0, NL, choose, 0)
 
     wait(c_copies)
     c_copies = []
@@ -283,8 +296,7 @@
             lambda o: hop_c.at[h, :, o], got_c.at[h, here[1 - h]], cs, cr, 2 + h, 1 - h
         )
         got_c[h, pl.ds(here[1 - h], 1)] = hop_c[h, :, pl.ds(here[1 - h], 1)].reshape(1, 8, 16, W)
-    words[...] = jnp.zeros((2, 64, 128), F32)
-    lax.fori_loop(0, NL, word, 0)
+    arrive(1)
     arrive(2)
     wait(n_copies)
     load_old.wait()
@@ -333,6 +345,7 @@
     fresh_in[pl.ds(m, 1)] = fresh[pl.ds(m, 1)]
     arrive(3)
     arrive(4)
+    arrive(5)
 
     wait(b_copies)
     b_copies = []
@@ -341,66 +354,100 @@
             lambda o: back_1.at[h, :, o], back_2.at[h, here[h]], bs, br, 2 + h, h
         )
         back_2[h, pl.ds(here[h], 1)] = back_1[h, :, pl.ds(here[h], 1)].reshape(1, 8, 16, W)
-    arrive(5)
     arrive(6)
     arrive(7)
     wait(b_copies)
 
-    def subtract(s, carry):
-        wanted = columns(metas[s, 32:33, :] + (2 * s).astype(F32))
-        pick = jnp.concatenate([hot(wanted == lane128 + 128.0 * t) for t in range(16)], axis=1)
-        anchor = dot(pick, back_2[...].reshape(2048, W)).astype(BF16)
-
-        def chunk_of(chunk, inner):
-            at = pl.ds(chunk * 8, 8)
-            near = dot(picks[s, at].reshape(256, W), anchor)
+    def read(chunk, carry):
+        at = pl.multiple_of(chunk * 256, 256)
+        found = dot(wants[pl.ds(at, 256), :], back_2[...].reshape(2048, W))
+        anchors[pl.ds(chunk * 2, 2)] = found.astype(BF16).reshape(2, 128, W)
+        return carry
+
+    lax.fori_loop(0, 4, read, 0)
+
+    def tabulate(to):
+        at = pl.ds(to * 8, 8)
+        for s in range(NL):
+            near = dot(picks[s, at].reshape(256, W), anchors[s])
             left = rows[s, at].reshape(256, W).astype(F32) - near
-            rows[s, at] = left.astype(BF16).reshape(8, 32, W)
-            return inner
-
-        return lax.fori_loop(0, 8, chunk_of, carry)
-
-    lax.fori_loop(0, NL, subtract, 0)
-
-    def tabulate(k, carry):
-        pick = jnp.concatenate(
-            [hot(words[g, pl.ds(k, 1), :] == sub128 + 1.0) for g in range(2)], axis=1
-        )
-        sums = dot(pick, rows[:, pl.ds(k, 1)].reshape(256, W)).astype(BF16)
-        across = lax.rem(k, 8) * 8 + lax.div(k, 8)
-        table[0, pl.ds(k, 1)] = sums[0:64].reshape(1, 64, W)
-        table[1, pl.ds(across, 1)] = sums[64:128].reshape(1, 64, W)
+            rest[:, 32 * s : 32 * s + 32, :] = left.astype(BF16).reshape(8, 32, W)
+        low = words[0, pl.ds(pl.multiple_of(to * 8, 8), 8), :]
+        high = words[1, pl.ds(pl.multiple_of(to * 8, 8), 8), :]
+        for k in range(8):
+            pick = jnp.concatenate(
+                [hot(w[k : k + 1] == sub128 + 1.0) for w in (low, high)], axis=1
+            )
+            sums = dot(pick, rest[k]).astype(BF16)
+            table[0, pl.ds(to * 8 + k, 1)] = sums[0:64].reshape(1, 64, W)
+            table[1, pl.ds(k * 8 + to, 1)] = sums[64:128].reshape(1, 64, W)
+
+    def first_a(d, start):
+        other, target = on_y(d)
+        return remote(
+            table.at[0, pl.ds(8 * other, 8)], table_1.at[0, y], ts.at[0, d], tr.at[0, d],
+            target, start,
+        )
+
+    def first_b(d, at, size, start):
+        other, target = on_z(d)
+        return remote(
+            table.at[1, pl.ds(8 * other + at, size)], table_1.at[1, z, pl.ds(at, size)],
+            ts.at[1, d], tr.at[1, d], target, start,
+        )
+
+    def send_group(i, carry):
+        far = lax.div(i + 1, 2)
+        d = 4 + far - 2 * far * lax.rem(i, 2)
+        to = lax.rem(y + d, NY)
+        tabulate(to)
+        first_a(d, True)
+        for e in range(1, 8):
+            first_b(e, to, 1, True)
         return carry
 
-    lax.fori_loop(0, 64, tabulate, 0)
-    t_copies = []
-    for h in range(2):
-        t_copies += spread(
-            lambda o: table.at[h, pl.ds(8 * o, 8)], table_1.at[h, here[h]], ts, tr, h, h
-        )
+    lax.fori_loop(0, 7, send_group, 0)
+    tabulate(y)
+    for e in range(1, 8):
+        first_b(e, y, 1, True)
+    for h in range(2):
         table_1[h, pl.ds(here[h], 1)] = table[h, pl.ds(8 * here[h], 8)].reshape(1, 8, 64, W)
     wait(v_copies)
     for s in range(NL):
         coarse_out[:, W * s : W * s + W] = fresh_in[s]
     column[...] = columns(jnp.sum(count_in[...], axis=0)[0:1])
-    wait(t_copies)
-
-    def gather(j, carry):
+    for d in range(1, 8):
+        first_a(d, False).wait()
+        first_b(d, 0, 8, False).wait()
+
+    def summed(h, j):
+        total = jnp.zeros((64, W), F32)
+        for i in range(8):
+            total = total + table_1[h, i, pl.ds(j, 1)].reshape(64, W).astype(F32)
+        return total.reshape(1, 64, W)
+
+    def second(h, d, start):
+        other, target = on[1 - h](d)
+        return remote(
+            part.at[h, other], part_2.at[h, here[1 - h]], ts.at[2 + h, d], tr.at[2 + h, d],
+            target, start,
+        )
+
+    def send_sums(i, carry):
+        far = lax.div(i + 1, 2)
+        d = 4 + far - 2 * far * lax.rem(i, 2)
         for h in range(2):
-            total = jnp.zeros((64, W), F32)
-            for i in range(8):
-                total = total + table_1[h, i, pl.ds(j, 1)].reshape(64, W).astype(F32)
-            part[h, pl.ds(j, 1)] = total.reshape(1, 64, W)
+            j = lax.rem(here[1 - h] + d, 8)
+            part[h, pl.ds(j, 1)] = summed(h, j)
+            second(h, d, True)
         return carry
 
-    lax.fori_loop(0, 8, gather, 0)
-    t_copies = []
-    for h in range(2):
-        t_copies += spread(
-            lambda o: part.at[h, o], part_2.at[h, here[1 - h]], ts, tr, 2 + h, 1 - h
-        )
-        part_2[h, pl.ds(here[1 - h], 1)] = part[h, pl.ds(here[1 - h], 1)]
-    wait(t_copies)
+    lax.fori_loop(0, 7, send_sums, 0)
+    for h in range(2):
+        part_2[h, pl.ds(here[1 - h], 1)] = summed(h, here[1 - h])
+    for d in range(1, 8):
+        for h in range(2):
+            second(h, d, False).wait()
     for h in range(2):
         total = jnp.sum(part_2[h], axis=0)
         for q in range(4):
@@ -443,7 +490,10 @@
             pltpu.VMEM((1024, 2 * W), BF16),
             pltpu.VMEM((NL, 64, 32, W), BF16),
             pltpu.VMEM((NL, 64, 32, W), BF16),
+            pltpu.VMEM((8, 256, W), BF16),
             pltpu.VMEM((2, 64, 128), F32),
+            pltpu.VMEM((1024, 2048), BF16),
+            pltpu.VMEM((NL, 128, W), BF16),
             pltpu.VMEM((128, 16, W), BF16),
             pltpu.VMEM((2, 8, 8, 16, W), BF16),
             pltpu.VMEM((2, 8, 8, 16, W), BF16),

time: 132 us -> 111 us (0.84)
  Pallas kernels: 128 us -> 107 us
    pallas_call x1, Pallas kernels: 128 us -> 107 us  [body(): pl.pallas_call(kernel, out_shape=(jax.ShapeDtypeStruct((64, 1024), F32),...]
where the time goes in v2:
time: 111 us; the launch traced here: 110 us
  Pallas kernels  107 us (96%)
  local copies, waits for them, and re-layouts  3.14 us (3%)
    pallas_call x1, Pallas kernels, body(): pl.pallas_call(kernel, out_shape=(jax.ShapeDtypeStruct((64, 1024), F32),...  107 us
    unnamed x2, local copies, waits for them, and re-layouts  3.14 us

profile of v2, /device:TPU:1, one launch (start us, length us, event | category | flops | bytes accessed | tf_op | source)
XLA Modules:
  0.0 110.5 jit_solution(382790534506736164)
XLA Ops:
  0.6 106.7 %shard_map.86 = (f32[64,1024]{1,0:T(8,128)}, f32[16,1024]{1,0:T(8,128)}) custom-call(bf16[1024,1024]{1,0:T(8,128)(2,1)} %frames_ref.1, s32[1,128]{1,0:T(1,128)} %length_ref.1, s32[1,128]{1,0:T(1,128)} %owner_ref.1, s32[1,128]{1,0:T(1,128)} %cluster_ref.1, s32[8,128]{1,0:T(8,128)} %bitcast.1, bf16[256,1024]{1,0:T(8,128)(2,1)} %old_ref.1, f32[16,1024]{1,0:T(8,128)} %old_codes_ref.1), custom_call_target="tpu_custom_call" | custom-call | tf_op jit(solution)/shard_map/pallas_call | solution.py:473
  107.3 1.7 %copy.11 = f32[64,1024]{1,0:T(8,128)} copy(f32[64,1024]{1,0:T(8,128)} %get-tuple-element.4) | data formatting | bytes 524288
  109.0 1.5 %copy.12 = f32[16,1024]{1,0:T(8,128)} copy(f32[16,1024]{1,0:T(8,128)} %get-tuple-element.5) | data formatting | bytes 131072

commit v3 on v2

--- a/solution.py
+++ b/solution.py
@@ -38,7 +38,7 @@
     frames_ref, length_ref, owner_ref, cluster_ref, code_ref, old_ref, old_codes_ref,
     coarse_out, codes_out,
     frames_v, mine, theirs, pooled, pool_in, old_v,
-    meta, metas, both, rows, picks, rest, words, wants, anchors,
+    video, videos, into, out_of, amount, meta, metas, both, rows, picks, rest, words, wants, anchors,
     send_c, hop_c, got_c, back_0, back_1, back_2,
     note_0, note_1, note_s, note_2, fresh, fresh_in,
     table, table_1, part, part_2, last, last_in, count, count_in, column,
@@ -129,13 +129,34 @@
     to_y = jnp.right_shift(owner_int, 4)
     to_z = jnp.bitwise_and(jnp.right_shift(owner_int, 1), NZ - 1)
     place = jnp.where(half == 0, to_y * NZ + to_z, to_z * NY + to_y)
-    meta[32:33, :] = (half * 1024 + place * 16).astype(F32) + repeat
-    meta[33:34, :] = cluster_ref[...].astype(F32) + 1.0
-    meta[34:35, :] = place.astype(F32)
-    meta[35:36, :] = repeat
-    meta[36:37, :] = half.astype(F32)
-    meta[37:40, :] = jnp.zeros((3, 128), F32)
-
+    video[0:1, :] = (half * 1024 + place * 16).astype(F32) + repeat
+    video[1:2, :] = cluster_ref[...].astype(F32) + 1.0
+    video[2:3, :] = place.astype(F32)
+    video[3:4, :] = repeat
+    video[4:5, :] = half.astype(F32)
+    video[5:8, :] = jnp.zeros((3, 128), F32)
+    videos[pl.ds(m, 1)] = video[...].reshape(1, 8, 128)
+
+    load.wait()
+    for j in range(8):
+        part_sum = dot(of_video, frames_v[:, 128 * j : 128 * j + 128])
+        pooled[j] = (part_sum / lengths).astype(BF16)
+    pl.semaphore_wait(barrier, 21)
+    x_copies, f_copies, p_copies = [], [], []
+    for d in range(1, 8):
+        other, target = member(d)
+        x_copies.append(remote(video, videos.at[m], xs.at[0, d], xr.at[0, d], target))
+    for d in range(1, 8):
+        other, target = member(d)
+        p_copies.append(
+            remote(pooled.at[other], pool_in.at[m], ps.at[d], pr.at[d], target)
+        )
+    partner = lax.rem(c + 1, 2)
+    old_copy = remote(
+        old_ref.at[:, pl.ds(pl.multiple_of((x * 2 + partner) * W, W), W)],
+        old_v.at[c], xs.at[0, 0], xr.at[0, 0],
+        {"dp": (y * NZ + z) * 2 + partner, "cent": x},
+    )
     codes = code_ref[...]
     line_of = jnp.right_shift(codes, 7).astype(F32)
     in_line = jnp.bitwise_and(codes, 127).astype(F32)
@@ -151,32 +172,15 @@
         seen = seen + dot(match, ones)
         histogram = histogram + dot_t(match, hot(in_line[a : a + 1] == sub128))
     meta[8:16, :] = in_line
-    meta[24:32, :] = line_of
-    metas[pl.ds(m, 1)] = meta[...].reshape(1, 40, 128)
+    metas[pl.ds(m, 1)] = meta[...].reshape(1, 24, 128)
     for j in range(8):
         note_0[0, j, 0:8, :] = histogram[8 * j : 8 * j + 8]
         note_0[1, j, 0:8, :] = jnp.zeros((8, 128), F32)
 
-    load.wait()
-    for j in range(8):
-        part_sum = dot(of_video, frames_v[:, 128 * j : 128 * j + 128])
-        pooled[j] = (part_sum / lengths).astype(BF16)
-    pl.semaphore_wait(barrier, 21)
-    x_copies, f_copies, p_copies = [], [], []
+    m_copies = []
     for d in range(1, 8):
         other, target = member(d)
-        x_copies.append(remote(meta, metas.at[m], xs.at[d], xr.at[d], target))
-    partner = lax.rem(c + 1, 2)
-    old_copy = remote(
-        old_ref.at[:, pl.ds(pl.multiple_of((x * 2 + partner) * W, W), W)],
-        old_v.at[c], xs.at[0], xr.at[0],
-        {"dp": (y * NZ + z) * 2 + partner, "cent": x},
-    )
-    for d in range(1, 8):
-        other, target = member(d)
-        p_copies.append(
-            remote(pooled.at[other], pool_in.at[m], ps.at[d], pr.at[d], target)
-        )
+        m_copies.append(remote(meta, metas.at[m], xs.at[1, d], xr.at[1, d], target))
     for d in range(1, 8):
         other, target = member(d)
         lanes = pl.ds(pl.multiple_of(other * W, W), W)
@@ -187,7 +191,7 @@
 
     wait(x_copies)
     places, values, halves, repeats = [
-        [metas[s, i : i + 1, :] for s in range(NL)] for i in (34, 33, 36, 35)
+        [videos[s, i : i + 1, :] for s in range(NL)] for i in (2, 1, 4, 3)
     ]
     note = []
     for h in range(2):
@@ -208,18 +212,18 @@
         note_1[h, pl.ds(here[h], 1)] = note_0[h, pl.ds(here[h], 1)]
 
     wait(p_copies)
-    sub256 = iota((256, 128), 0)
+    sub256, sub512 = iota((256, 128), 0), iota((512, 128), 0)
 
     def fill(chunk, carry):
-        shift = (chunk * 256).astype(F32)
+        shift = (chunk * 512).astype(F32)
         pick = jnp.concatenate(
-            [hot(metas[s, 32:33, :] + 2.0 * s - shift == sub256) for s in range(NL)], axis=1
+            [hot(videos[s, 0:1, :] + 2.0 * s - shift == sub512) for s in range(NL)], axis=1
         )
         filled = dot(pick, pool_in[...].reshape(1024, W))
-        send_c[pl.ds(chunk * 16, 16)] = filled.astype(BF16).reshape(16, 16, W)
+        send_c[pl.ds(chunk * 32, 32)] = filled.astype(BF16).reshape(32, 16, W)
         return carry
 
-    lax.fori_loop(0, 8, fill, 0)
+    lax.fori_loop(0, 4, fill, 0)
     c_copies = []
     for h in range(2):
         c_copies += spread(
@@ -246,16 +250,16 @@
         both[:, :W] = theirs[s]
 
         def chunk_of(chunk, carry):
-            shift = (chunk * 256).astype(F32)
+            shift = (chunk * 512).astype(F32)
             pick = jnp.concatenate(
-                [hot(metas[s, a : a + 1, :] - shift == sub256) for a in range(8)], axis=1
+                [hot(metas[s, a : a + 1, :] - shift == sub512) for a in range(8)], axis=1
             )
             out = dot(pick, both[...]).astype(BF16)
-            rows[s, pl.ds(chunk * 8, 8)] = out[:, :W].reshape(8, 32, W)
-            picks[s, pl.ds(chunk * 8, 8)] = out[:, W:].reshape(8, 32, W)
+            rows[s, pl.ds(chunk * 16, 16)] = out[:, :W].reshape(16, 32, W)
+            picks[s, pl.ds(chunk * 16, 16)] = out[:, W:].reshape(16, 32, W)
             return carry
 
-        lax.fori_loop(0, 8, chunk_of, 0)
+        lax.fori_loop(0, 4, chunk_of, 0)
 
     def arrive(d):
         if d == 0:
@@ -268,8 +272,9 @@
         offset = (lax.rem(s, 4) * 32).astype(F32)
         values, ranks = [], []
         for a in range(8):
-            line = metas[s, 24 + a : 25 + a, :]
-            rank = metas[s, a : a + 1, :] - 32.0 * line + offset
+            slot = metas[s, a : a + 1, :]
+            line = jnp.floor(slot * (1.0 / 32.0))
+            rank = slot - 32.0 * line + offset
             value = metas[s, 8 + a : 9 + a, :] + 1.0
             values.append(jnp.where(line == sub64, value, 0.0).astype(BF16))
             ranks.append(hot(rank == sub128))
@@ -279,12 +284,13 @@
         return carry
 
     def choose(s, carry):
-        wanted = columns(metas[s, 32:33, :] + (2 * s).astype(F32))
+        wanted = columns(videos[s, 0:1, :] + (2 * s).astype(F32))
         pick = [hot(wanted == lane128 + 128.0 * t) for t in range(16)]
         wants[pl.ds(pl.multiple_of(s * 128, 128), 128), :] = jnp.concatenate(pick, axis=1)
         return carry
 
     arrive(0)
+    wait(m_copies)
     words[...] = jnp.zeros((2, 64, 128), F32)
     lax.fori_loop(0, NL, word, 0)
     lax.fori_loop(0, NL, choose, 0)
@@ -296,15 +302,8 @@
             lambda o: hop_c.at[h, :, o], got_c.at[h, here[1 - h]], cs, cr, 2 + h, 1 - h
         )
         got_c[h, pl.ds(here[1 - h], 1)] = hop_c[h, :, pl.ds(here[1 - h], 1)].reshape(1, 8, 16, W)
-    arrive(1)
-    arrive(2)
     wait(n_copies)
-    load_old.wait()
-    old_copy.wait()
-    wait(c_copies)
-
-    sub8 = iota((8, 128), 0)
-    b_copies, v_copies = [], []
+    sub8, lane256 = iota((8, 128), 0), iota((128, 256), 1)
     for h in range(2):
         mask = sub8 == here[1 - h].astype(F32)
         ids = [
@@ -312,21 +311,12 @@
             for j in range(8)
         ]
         pick = jnp.concatenate([hot(ids[j] == sub256 + 1.0) for j in range(8)], axis=1)
-        total = dot(pick, got_c[h].reshape(1024, W))
-        amount = dot(pick, jnp.ones((1024, W), BF16))
-        new = (total + old_v[h].astype(F32)) / (amount + 1.0)
-        for q in range(4):
-            fresh[2 * q + h] = new[64 * q : 64 * q + 64]
-        anchor = new.astype(BF16)
-        lane256 = iota((128, 256), 1)
+        into[h] = pick
+        amount[h] = dot(pick, jnp.ones((1024, W), BF16)) + 1.0
         for j in range(8):
             column_of = columns(ids[j])
-            back = hot(jnp.concatenate([column_of, column_of], axis=1) == lane256 + 1.0)
-            back_0[h, j] = dot(back, anchor).astype(BF16).reshape(8, 16, W)
-        b_copies += spread(
-            lambda o: back_0.at[h, o], back_1.at[h, here[1 - h]], bs, br, h, 1 - h
-        )
-        back_1[h, pl.ds(here[1 - h], 1)] = back_0[h, pl.ds(here[1 - h], 1)]
+            back = jnp.concatenate([column_of, column_of], axis=1) == lane256 + 1.0
+            out_of[h, 128 * j : 128 * j + 128, :] = hot(back)
     counts = jnp.zeros((1, 128), F32)
     for j in range(8):
         counts = counts + jnp.sum(
@@ -334,6 +324,26 @@
         )
     count[...] = jnp.broadcast_to(counts, (8, 128))
     count_in[pl.ds(m, 1)] = count[...].reshape(1, 8, 128)
+    arrive(1)
+    arrive(2)
+    load_old.wait()
+    old_copy.wait()
+    wait(c_copies)
+
+    b_copies, v_copies, fresh_of = [], [], []
+    for h in range(2):
+        total = dot(into[h], got_c[h].reshape(1024, W))
+        fresh_of.append((total + old_v[h].astype(F32)) / amount[h])
+    for h in range(2):
+        found = dot(out_of[h], fresh_of[h].astype(BF16)).astype(BF16)
+        back_0[h] = found.reshape(8, 8, 16, W)
+        b_copies += spread(
+            lambda o: back_0.at[h, o], back_1.at[h, here[1 - h]], bs, br, h, 1 - h
+        )
+        back_1[h, pl.ds(here[1 - h], 1)] = back_0[h, pl.ds(here[1 - h], 1)]
+    for h in range(2):
+        for q in range(4):
+            fresh[2 * q + h] = fresh_of[h][64 * q : 64 * q + 64]
     for d in range(1, 8):
         other, target = member(d)
         v_copies.append(
@@ -466,11 +476,16 @@
         codes_out[:, lanes] = (last_in[s] + code_prior * old_codes_ref[:, lanes]) / mine[...]
 
 
+def hand_on(coarse_in, codes_in, coarse_out, codes_out):
+    coarse_out[...] = coarse_in[...]
+    codes_out[...] = codes_in[...]
+
+
 def body(frames, video_length, video_owner, video_cluster, frame_code, old_coarse, old_codes):
     dma = pltpu.SemaphoreType.DMA
     vmem = pl.BlockSpec(memory_space=pltpu.VMEM)
     hbm = pl.BlockSpec(memory_space=pl.ANY)
-    return pl.pallas_call(
+    coarse, codes = pl.pallas_call(
         kernel,
         out_shape=(
             jax.ShapeDtypeStruct((64, 1024), F32),
@@ -485,8 +500,13 @@
             pltpu.VMEM((NL, 128, W), BF16),
             pltpu.VMEM((NL, 128, W), BF16),
             pltpu.VMEM((2, 256, W), BF16),
-            pltpu.VMEM((40, 128), F32),
-            pltpu.VMEM((NL, 40, 128), F32),
+            pltpu.VMEM((8, 128), F32),
+            pltpu.VMEM((NL, 8, 128), F32),
+            pltpu.VMEM((2, 256, 1024), BF16),
+            pltpu.VMEM((2, 1024, 256), BF16),
+            pltpu.VMEM((2, 256, W), F32),
+            pltpu.VMEM((24, 128), F32),
+            pltpu.VMEM((NL, 24, 128), F32),
             pltpu.VMEM((1024, 2 * W), BF16),
             pltpu.VMEM((NL, 64, 32, W), BF16),
             pltpu.VMEM((NL, 64, 32, W), BF16),
@@ -516,7 +536,7 @@
             pltpu.VMEM((NL, 8, 128), F32),
             pltpu.VMEM((128, 128), F32),
             dma((3,)),
-            dma((8,)), dma((8,)),
+            dma((2, 8)), dma((2, 8)),
             dma((8,)), dma((8,)),
             dma((8,)), dma((8,)),
             dma((4, 8)), dma((4, 8)),
@@ -532,6 +552,15 @@
         frames, video_length, video_owner, video_cluster,
         frame_code.reshape(8, 128), old_coarse, old_codes,
     )
+    return pl.pallas_call(
+        hand_on,
+        out_shape=(
+            jax.ShapeDtypeStruct((64, 1024), F32),
+            jax.ShapeDtypeStruct((16, 1024), F32),
+        ),
+        in_specs=[vmem, vmem],
+        out_specs=(vmem, vmem),
+    )(coarse, codes)
 
 
 def solution(mesh):

time: 111 us -> 106 us (0.955)
  local copies, waits for them, and re-layouts: 3.14 us -> 0 us
  Pallas kernels: 107 us -> 105 us
    pallas_call x1, Pallas kernels: 107 us -> 103 us  [body(): pl.pallas_call(kernel, out_shape=(jax.ShapeDtypeStruct((64, 1024), F32),...]
    unnamed x2 -> x0, local copies, waits for them, and re-layouts: 3.14 us -> none
    pallas_call x0 -> x1, Pallas kernels: none -> 1.69 us  [body(): pl.pallas_call(hand_on, out_shape=(jax.ShapeDtypeStruct((64, 1024), F32),...]
where the time goes in v3:
time: 106 us; the launch traced here: 105 us
  Pallas kernels  105 us (99%)
    pallas_call x1, Pallas kernels, body(): pl.pallas_call(kernel, out_shape=(jax.ShapeDtypeStruct((64, 1024), F32),...  103 us

profile of v3, /device:TPU:1, one launch (start us, length us, event | category | flops | bytes accessed | tf_op | source)
XLA Modules:
  0.0 105.3 jit_solution(17167565706277718270)
XLA Ops:
  0.6 103.0 %shard_map.86 = (f32[64,1024]{1,0:T(8,128)}, f32[16,1024]{1,0:T(8,128)}) custom-call(bf16[1024,1024]{1,0:T(8,128)(2,1)} %frames_ref.1, s32[1,128]{1,0:T(1,128)} %length_ref.1, s32[1,128]{1,0:T(1,128)} %owner_ref.1, s32[1,128]{1,0:T(1,128)} %cluster_ref.1, s32[8,128]{1,0:T(8,128)} %bitcast.1, bf16[256,1024]{1,0:T(8,128)(2,1)} %old_ref.1, f32[16,1024]{1,0:T(8,128)} %old_codes_ref.1), custom_call_target="tpu_custom_call" | custom-call | tf_op jit(solution)/shard_map/pallas_call | solution.py:488
  103.6 1.7 %shard_map.87 = (f32[64,1024]{1,0:T(8,128)}, f32[16,1024]{1,0:T(8,128)}) custom-call(f32[64,1024]{1,0:T(8,128)} %get-tuple-element.4.coarse_in, f32[16,1024]{1,0:T(8,128)} %get-tuple-element.5.codes_in), custom_call_target="tpu_custom_call" | custom-call | tf_op jit(solution)/shard_map/pallas_call | solution.py:555

commit v4 on v3

--- a/solution.py
+++ b/solution.py
@@ -38,7 +38,7 @@
     frames_ref, length_ref, owner_ref, cluster_ref, code_ref, old_ref, old_codes_ref,
     coarse_out, codes_out,
     frames_v, mine, theirs, pooled, pool_in, old_v,
-    video, videos, into, out_of, amount, meta, metas, both, rows, picks, rest, words, wants, anchors,
+    video, videos, into, out_of, amount, meta, metas, both, rows, picks, rest, words, wants, wide, anchors,
     send_c, hop_c, got_c, back_0, back_1, back_2,
     note_0, note_1, note_s, note_2, fresh, fresh_in,
     table, table_1, part, part_2, last, last_in, count, count_in, column,
@@ -99,9 +99,12 @@
             )
 
     my_lanes = pl.ds(pl.multiple_of(m * W, W), W)
-    load = local(frames_ref, frames_v, load_sem.at[0])
-    load_mine = local(frames_ref.at[:, my_lanes], theirs.at[m], load_sem.at[1])
-    load_old = local(old_ref.at[:, my_lanes], old_v.at[c], load_sem.at[2])
+    loads = []
+    for d in range(1, 8):
+        lanes = pl.ds(pl.multiple_of(member(d)[0] * W, W), W)
+        loads.append(local(frames_ref.at[:, lanes], frames_v.at[d], load_sem.at[d]))
+    load_mine = local(frames_ref.at[:, my_lanes], theirs.at[m], load_sem.at[0])
+    load_old = local(old_ref.at[:, my_lanes], old_v.at[c], load_sem.at[8])
 
     sub128, lane128 = iota((128, 128), 0), iota((128, 128), 1)
     sub64 = iota((64, 128), 0)
@@ -137,10 +140,6 @@
     video[5:8, :] = jnp.zeros((3, 128), F32)
     videos[pl.ds(m, 1)] = video[...].reshape(1, 8, 128)
 
-    load.wait()
-    for j in range(8):
-        part_sum = dot(of_video, frames_v[:, 128 * j : 128 * j + 128])
-        pooled[j] = (part_sum / lengths).astype(BF16)
     pl.semaphore_wait(barrier, 21)
     x_copies, f_copies, p_copies = [], [], []
     for d in range(1, 8):
@@ -148,8 +147,10 @@
         x_copies.append(remote(video, videos.at[m], xs.at[0, d], xr.at[0, d], target))
     for d in range(1, 8):
         other, target = member(d)
+        loads[d - 1].wait()
+        pooled[d] = (dot(of_video, frames_v[d]) / lengths).astype(BF16)
         p_copies.append(
-            remote(pooled.at[other], pool_in.at[m], ps.at[d], pr.at[d], target)
+            remote(pooled.at[d], pool_in.at[m], ps.at[d], pr.at[d], target)
         )
     partner = lax.rem(c + 1, 2)
     old_copy = remote(
@@ -183,11 +184,12 @@
         m_copies.append(remote(meta, metas.at[m], xs.at[1, d], xr.at[1, d], target))
     for d in range(1, 8):
         other, target = member(d)
-        lanes = pl.ds(pl.multiple_of(other * W, W), W)
         f_copies.append(
-            remote(frames_ref.at[:, lanes], theirs.at[m], fs.at[d], fr.at[d], target)
-        )
-    pool_in[pl.ds(m, 1)] = pooled[pl.ds(m, 1)]
+            remote(frames_v.at[d], theirs.at[m], fs.at[d], fr.at[d], target)
+        )
+    load_mine.wait()
+    own = dot(of_video, theirs[pl.ds(m, 1)].reshape(1024, W)) / lengths
+    pool_in[pl.ds(m, 1)] = own.astype(BF16).reshape(1, 128, W)
 
     wait(x_copies)
     places, values, halves, repeats = [
@@ -262,9 +264,7 @@
         lax.fori_loop(0, 4, chunk_of, 0)
 
     def arrive(d):
-        if d == 0:
-            load_mine.wait()
-        else:
+        if d > 0:
             f_copies[d - 1].wait()
         take(d)
 
@@ -284,9 +284,10 @@
         return carry
 
     def choose(s, carry):
-        wanted = columns(videos[s, 0:1, :] + (2 * s).astype(F32))
-        pick = [hot(wanted == lane128 + 128.0 * t) for t in range(16)]
-        wants[pl.ds(pl.multiple_of(s * 128, 128), 128), :] = jnp.concatenate(pick, axis=1)
+        info = videos[s]
+        wanted = columns(info[3:4] * 128.0 + info[4:5] * 64.0 + info[2:3])
+        pick = [hot(wanted == lane128 + 128.0 * t) for t in range(2)]
+        wants[pl.ds(s, 1)] = jnp.concatenate(pick, axis=1).reshape(1, 128, 256)
         return carry
 
     arrive(0)
@@ -325,7 +326,6 @@
     count[...] = jnp.broadcast_to(counts, (8, 128))
     count_in[pl.ds(m, 1)] = count[...].reshape(1, 8, 128)
     arrive(1)
-    arrive(2)
     load_old.wait()
     old_copy.wait()
     wait(c_copies)
@@ -353,9 +353,9 @@
             remote(count, count_in.at[m], es.at[1, d], er.at[1, d], target)
         )
     fresh_in[pl.ds(m, 1)] = fresh[pl.ds(m, 1)]
+    arrive(2)
     arrive(3)
     arrive(4)
-    arrive(5)
 
     wait(b_copies)
     b_copies = []
@@ -364,17 +364,15 @@
             lambda o: back_1.at[h, :, o], back_2.at[h, here[h]], bs, br, 2 + h, h
         )
         back_2[h, pl.ds(here[h], 1)] = back_1[h, :, pl.ds(here[h], 1)].reshape(1, 8, 16, W)
+    arrive(5)
     arrive(6)
     arrive(7)
     wait(b_copies)
 
-    def read(chunk, carry):
-        at = pl.multiple_of(chunk * 256, 256)
-        found = dot(wants[pl.ds(at, 256), :], back_2[...].reshape(2048, W))
-        anchors[pl.ds(chunk * 2, 2)] = found.astype(BF16).reshape(2, 128, W)
-        return carry
-
-    lax.fori_loop(0, 4, read, 0)
+    wide[...] = back_2[...].reshape(2048, W).astype(F32)
+    for s in range(NL):
+        found = [wide[pl.ds(2 * s + r, 128, stride=16), :].astype(BF16) for r in range(2)]
+        anchors[s] = dot(wants[s], jnp.concatenate(found, axis=0)).astype(BF16)
 
     def tabulate(to):
         at = pl.ds(to * 8, 8)
@@ -494,7 +492,7 @@
         in_specs=[hbm, vmem, vmem, vmem, vmem, hbm, vmem],
         out_specs=(vmem, vmem),
         scratch_shapes=[
-            pltpu.VMEM((1024, 1024), BF16),
+            pltpu.VMEM((NL, 1024, W), BF16),
             pltpu.VMEM((16, 128), F32),
             pltpu.VMEM((NL, 1024, W), BF16),
             pltpu.VMEM((NL, 128, W), BF16),
@@ -512,7 +510,8 @@
             pltpu.VMEM((NL, 64, 32, W), BF16),
             pltpu.VMEM((8, 256, W), BF16),
             pltpu.VMEM((2, 64, 128), F32),
-            pltpu.VMEM((1024, 2048), BF16),
+            pltpu.VMEM((NL, 128, 256), BF16),
+            pltpu.VMEM((2048, W), F32),
             pltpu.VMEM((NL, 128, W), BF16),
             pltpu.VMEM((128, 16, W), BF16),
             pltpu.VMEM((2, 8, 8, 16, W), BF16),
@@ -535,7 +534,7 @@
             pltpu.VMEM((8, 128), F32),
             pltpu.VMEM((NL, 8, 128), F32),
             pltpu.VMEM((128, 128), F32),
-            dma((3,)),
+            dma((9,)),
             dma((2, 8)), dma((2, 8)),
             dma((8,)), dma((8,)),
             dma((8,)), dma((8,)),

time: 106 us -> 107 us (level)
    pallas_call x1, Pallas kernels: 103 us -> 104 us  [body(): pl.pallas_call(kernel, out_shape=(jax.ShapeDtypeStruct((64, 1024), F32),...]
where the time goes in v4:
time: 107 us
  Pallas kernels  106 us (99%)
    pallas_call x1, Pallas kernels, body(): pl.pallas_call(kernel, out_shape=(jax.ShapeDtypeStruct((64, 1024), F32),...  104 us

profile of v4, /device:TPU:1, one launch (start us, length us, event | category | flops | bytes accessed | tf_op | source)
XLA Modules:
  0.0 106.5 jit_solution(5508906708339536454)
XLA Ops:
  0.6 104.2 %shard_map.86 = (f32[64,1024]{1,0:T(8,128)}, f32[16,1024]{1,0:T(8,128)}) custom-call(bf16[1024,1024]{1,0:T(8,128)(2,1)} %frames_ref.1, s32[1,128]{1,0:T(1,128)} %length_ref.1, s32[1,128]{1,0:T(1,128)} %owner_ref.1, s32[1,128]{1,0:T(1,128)} %cluster_ref.1, s32[8,128]{1,0:T(8,128)} %bitcast.1, bf16[256,1024]{1,0:T(8,128)(2,1)} %old_ref.1, f32[16,1024]{1,0:T(8,128)} %old_codes_ref.1), custom_call_target="tpu_custom_call" | custom-call | tf_op jit(solution)/shard_map/pallas_call | solution.py:486
  104.8 1.7 %shard_map.87 = (f32[64,1024]{1,0:T(8,128)}, f32[16,1024]{1,0:T(8,128)}) custom-call(f32[64,1024]{1,0:T(8,128)} %get-tuple-element.4.coarse_in, f32[16,1024]{1,0:T(8,128)} %get-tuple-element.5.codes_in), custom_call_target="tpu_custom_call" | custom-call | tf_op jit(solution)/shard_map/pallas_call | solution.py:554

commit v5 on v3

--- a/solution.py
+++ b/solution.py
@@ -10,6 +10,7 @@
 NY = 8
 NZ = 8
 W = 128
+FAR = (4, 3, 5, 2, 6, 1, 7)
 F32 = jnp.float32
 BF16 = jnp.bfloat16
 
@@ -38,7 +39,7 @@
     frames_ref, length_ref, owner_ref, cluster_ref, code_ref, old_ref, old_codes_ref,
     coarse_out, codes_out,
     frames_v, mine, theirs, pooled, pool_in, old_v,
-    video, videos, into, out_of, amount, meta, metas, both, rows, picks, rest, words, wants, anchors,
+    video, videos, into, out_of, amount, meta, metas, both, rows, picks, rest, words, wants, wide, anchors,
     send_c, hop_c, got_c, back_0, back_1, back_2,
     note_0, note_1, note_s, note_2, fresh, fresh_in,
     table, table_1, part, part_2, last, last_in, count, count_in, column,
@@ -86,7 +87,7 @@
 
     def spread(src, dst, send, recv, stage, axis):
         copies = []
-        for d in range(1, 8):
+        for d in FAR:
             other, target = on[axis](d)
             copies.append(remote(src(other), dst, send.at[stage, d], recv.at[stage, d], target))
         return copies
@@ -284,9 +285,10 @@
         return carry
 
     def choose(s, carry):
-        wanted = columns(videos[s, 0:1, :] + (2 * s).astype(F32))
-        pick = [hot(wanted == lane128 + 128.0 * t) for t in range(16)]
-        wants[pl.ds(pl.multiple_of(s * 128, 128), 128), :] = jnp.concatenate(pick, axis=1)
+        info = videos[s]
+        wanted = columns(info[3:4] * 128.0 + info[4:5] * 64.0 + info[2:3])
+        pick = [hot(wanted == lane128 + 128.0 * t) for t in range(2)]
+        wants[pl.ds(s, 1)] = jnp.concatenate(pick, axis=1).reshape(1, 128, 256)
         return carry
 
     arrive(0)
@@ -325,7 +327,6 @@
     count[...] = jnp.broadcast_to(counts, (8, 128))
     count_in[pl.ds(m, 1)] = count[...].reshape(1, 8, 128)
     arrive(1)
-    arrive(2)
     load_old.wait()
     old_copy.wait()
     wait(c_copies)
@@ -353,9 +354,9 @@
             remote(count, count_in.at[m], es.at[1, d], er.at[1, d], target)
         )
     fresh_in[pl.ds(m, 1)] = fresh[pl.ds(m, 1)]
+    arrive(2)
     arrive(3)
     arrive(4)
-    arrive(5)
 
     wait(b_copies)
     b_copies = []
@@ -364,17 +365,15 @@
             lambda o: back_1.at[h, :, o], back_2.at[h, here[h]], bs, br, 2 + h, h
         )
         back_2[h, pl.ds(here[h], 1)] = back_1[h, :, pl.ds(here[h], 1)].reshape(1, 8, 16, W)
+    arrive(5)
     arrive(6)
     arrive(7)
     wait(b_copies)
 
-    def read(chunk, carry):
-        at = pl.multiple_of(chunk * 256, 256)
-        found = dot(wants[pl.ds(at, 256), :], back_2[...].reshape(2048, W))
-        anchors[pl.ds(chunk * 2, 2)] = found.astype(BF16).reshape(2, 128, W)
-        return carry
-
-    lax.fori_loop(0, 4, read, 0)
+    wide[...] = back_2[...].reshape(2048, W).astype(F32)
+    for s in range(NL):
+        found = [wide[pl.ds(2 * s + r, 128, stride=16), :].astype(BF16) for r in range(2)]
+        anchors[s] = dot(wants[s], jnp.concatenate(found, axis=0)).astype(BF16)
 
     def tabulate(to):
         at = pl.ds(to * 8, 8)
@@ -412,13 +411,13 @@
         to = lax.rem(y + d, NY)
         tabulate(to)
         first_a(d, True)
-        for e in range(1, 8):
+        for e in FAR:
             first_b(e, to, 1, True)
         return carry
 
     lax.fori_loop(0, 7, send_group, 0)
     tabulate(y)
-    for e in range(1, 8):
+    for e in FAR:
         first_b(e, y, 1, True)
     for h in range(2):
         table_1[h, pl.ds(here[h], 1)] = table[h, pl.ds(8 * here[h], 8)].reshape(1, 8, 64, W)
@@ -512,7 +511,8 @@
             pltpu.VMEM((NL, 64, 32, W), BF16),
             pltpu.VMEM((8, 256, W), BF16),
             pltpu.VMEM((2, 64, 128), F32),
-            pltpu.VMEM((1024, 2048), BF16),
+            pltpu.VMEM((NL, 128, 256), BF16),
+            pltpu.VMEM((2048, W), F32),
             pltpu.VMEM((NL, 128, W), BF16),
             pltpu.VMEM((128, 16, W), BF16),
             pltpu.VMEM((2, 8, 8, 16, W), BF16),

time: 106 us -> 102 us (0.962)
  Pallas kernels: 105 us -> 101 us
    pallas_call x1, Pallas kernels: 103 us -> 99.6 us  [body(): pl.pallas_call(kernel, out_shape=(jax.ShapeDtypeStruct((64, 1024), F32),...]
where the time goes in v5:
time: 102 us
  Pallas kernels  101 us (99%)
    pallas_call x1, Pallas kernels, body(): pl.pallas_call(kernel, out_shape=(jax.ShapeDtypeStruct((64, 1024), F32),...  99.6 us

profile of v5, /device:TPU:1, one launch (start us, length us, event | category | flops | bytes accessed | tf_op | source)
XLA Modules:
  0.0 102.0 jit_solution(6239188596847432049)
XLA Ops:
  0.6 99.6 %shard_map.86 = (f32[64,1024]{1,0:T(8,128)}, f32[16,1024]{1,0:T(8,128)}) custom-call(bf16[1024,1024]{1,0:T(8,128)(2,1)} %frames_ref.1, s32[1,128]{1,0:T(1,128)} %length_ref.1, s32[1,128]{1,0:T(1,128)} %owner_ref.1, s32[1,128]{1,0:T(1,128)} %cluster_ref.1, s32[8,128]{1,0:T(8,128)} %bitcast.1, bf16[256,1024]{1,0:T(8,128)(2,1)} %old_ref.1, f32[16,1024]{1,0:T(8,128)} %old_codes_ref.1), custom_call_target="tpu_custom_call" | custom-call | tf_op jit(solution)/shard_map/pallas_call | solution.py:487
  100.3 1.7 %shard_map.87 = (f32[64,1024]{1,0:T(8,128)}, f32[16,1024]{1,0:T(8,128)}) custom-call(f32[64,1024]{1,0:T(8,128)} %get-tuple-element.4.coarse_in, f32[16,1024]{1,0:T(8,128)} %get-tuple-element.5.codes_in), custom_call_target="tpu_custom_call" | custom-call | tf_op jit(solution)/shard_map/pallas_call | solution.py:555

commit v6 on v5

--- a/solution.py
+++ b/solution.py
@@ -93,7 +93,7 @@
         return copies
 
     barrier = pltpu.get_barrier_semaphore()
-    for d in range(1, 8):
+    for d in FAR:
         for find in (member, on_y, on_z):
             pl.semaphore_signal(
                 barrier, inc=1, device_id=find(d)[1], device_id_type=pl.DeviceIdType.MESH
@@ -224,9 +224,9 @@
         send_c[pl.ds(chunk * 32, 32)] = filled.astype(BF16).reshape(32, 16, W)
         return carry
 
-    lax.fori_loop(0, 4, fill, 0)
     c_copies = []
     for h in range(2):
+        lax.fori_loop(2 * h, 2 * h + 2, fill, 0)
         c_copies += spread(
             lambda o: send_c.at[pl.ds(64 * h + 8 * o, 8)], hop_c.at[h, here[h]], cs, cr, h, h
         )

time: 102 us -> 102 us (level)
  no operation moved by 1% of the time
where the time goes in v6:
time: 102 us
  Pallas kernels  101 us (99%)
    pallas_call x1, Pallas kernels, body(): pl.pallas_call(kernel, out_shape=(jax.ShapeDtypeStruct((64, 1024), F32),...  99.8 us

profile of v6, /device:TPU:1, one launch (start us, length us, event | category | flops | bytes accessed | tf_op | source)
XLA Modules:
  0.0 102.1 jit_solution(16417494419527533951)
XLA Ops:
  0.6 99.8 %shard_map.86 = (f32[64,1024]{1,0:T(8,128)}, f32[16,1024]{1,0:T(8,128)}) custom-call(bf16[1024,1024]{1,0:T(8,128)(2,1)} %frames_ref.1, s32[1,128]{1,0:T(1,128)} %length_ref.1, s32[1,128]{1,0:T(1,128)} %owner_ref.1, s32[1,128]{1,0:T(1,128)} %cluster_ref.1, s32[8,128]{1,0:T(8,128)} %bitcast.1, bf16[256,1024]{1,0:T(8,128)(2,1)} %old_ref.1, f32[16,1024]{1,0:T(8,128)} %old_codes_ref.1), custom_call_target="tpu_custom_call" | custom-call | tf_op jit(solution)/shard_map/pallas_call | solution.py:487
  100.4 1.7 %shard_map.87 = (f32[64,1024]{1,0:T(8,128)}, f32[16,1024]{1,0:T(8,128)}) custom-call(f32[64,1024]{1,0:T(8,128)} %get-tuple-element.4.coarse_in, f32[16,1024]{1,0:T(8,128)} %get-tuple-element.5.codes_in), custom_call_target="tpu_custom_call" | custom-call | tf_op jit(solution)/shard_map/pallas_call | solution.py:555
